TPU v7x, 256 devices: a whole 4x4x8 slice. The times are simulated.
256 devices in a mesh: group: 2 (over z_hi), ctx: 16 (over z_lo, y), tp: 8 (over x, core).
Axes of the slice: x: 4, y: 4, z: 8 (z_hi: 2, z_lo: 4; z = z_hi * 4 + z_lo), core: 2. Of those that a mesh axis runs over, the one named last changes fastest.
Arguments:
- stretch_query: bfloat16 [2, 2048, 8192], P('group', 'ctx', 'tp'), may hold values from -8 to 8
- prefix_keyvals: bfloat16 [2, 2, 16384, 1024], P('group', None, 'ctx', 'tp'), may hold values from -6 to 6
- stretch_key_values: bfloat16 [2, 2, 2048, 1024], P('group', None, 'ctx', 'tp'), may hold values from -6 to 6
- stretch_start: int32 [2], P('group'), may hold values from 4096 to 16384
- decode_query: bfloat16 [512, 4, 8192], P(('group', 'ctx'), None, 'tp'), may hold values from -8 to 8
- draft_key_values: bfloat16 [2, 512, 4, 1024], P(None, ('group', 'ctx'), None, 'tp'), may hold values from -6 to 6
- decode_cache: bfloat16 [2, 512, 1024, 1024], P(None, ('group', 'ctx'), None, 'tp'), may hold values from -6 to 6
- cache_lengths: int32 [512], P(('group', 'ctx')), may hold values from 128 to 1024, as said below
- page_rows: int32 [32], replicated, may hold values from 0 to 511, as said below
Outputs:
- prefill_out: bfloat16 [2, 2048, 8192], P('group', 'ctx', 'tp')
- decode_out: bfloat16 [512, 4, 8192], P(('group', 'ctx'), None, 'tp')
Inputs may be any that keep to these rules, and one draw needn't show every extreme that they name: `cache_lengths`: one row has length 1024. `page_rows`: page n = g * 16 + c names one of the rows m * 16 to m * 16 + 15, where m = (n + 1) mod 32 if n mod 4 = 1, m = g * 16 + (c + 16 / 2) mod 16 if n mod 4 = 3, and m = (n + 16) mod 32 for even n; no row is named twice.
All inputs are finite; a program needn't handle non-finite values.
Results may differ from a plain program's by a relative error of at most 0.0049.
Values may be sent and summed in bfloat16 or wider, within the bound.
No kernel may reach another device: no remote copies, remote signals or barrier semaphores. Data moves between devices by JAX's collectives and lax.ppermute only.
A program may use at most 128 MiB of HBM per device.

v0:
```python
import math
import jax
import jax.numpy as jnp
from jax import lax
from jax.sharding import PartitionSpec as P

QUERY_HEADS = 64
KEY_VALUE_HEADS = 8
HEAD_SIZE = 128


def joined_along(tiles, dim):
    lengths = list(tiles.shape[1:])
    lengths[dim] *= tiles.shape[0]
    return jnp.moveaxis(tiles, 0, dim).reshape(lengths)


def copy_for_each(x, axis):
    copies = jnp.broadcast_to(x, (lax.axis_size(axis), *x.shape))
    return lax.all_to_all(copies, axis, split_axis=0, concat_axis=0, tiled=True)


def gather_directly(x, axis, dim):
    return joined_along(copy_for_each(x, axis), dim)


def refresh(maxima, totals, scores, allowed):
    masked = jnp.where(allowed, scores, -jnp.inf)
    highest = jnp.maximum(maxima, jnp.max(masked, axis=-1))
    anchor = jnp.where(highest == -jnp.inf, 0.0, highest)
    weights = jnp.exp(masked - anchor[..., None])
    factor = jnp.exp(maxima - anchor)
    totals = totals * factor + jnp.sum(weights, axis=-1)
    return (highest, totals, weights.astype(jnp.bfloat16), factor)


def prefill_folder(queries, query_pos, limit, causal, inv_root, running, shard_piece):
    heads_local = queries.shape[1]
    piece_rows = shard_piece.shape[2]
    block_size = 512

    def absorb_step(block_index, carry):
        maxima, totals, summed = carry
        offset = block_index * block_size
        block = lax.dynamic_slice_in_dim(shard_piece, offset, block_size, 2)
        key_block = block[0, 0].reshape(block_size, heads_local, HEAD_SIZE)
        value_block = block[0, 1].reshape(block_size, heads_local, HEAD_SIZE)
        scores = (
            jnp.einsum("tkgd,skd->kgts", queries, key_block, preferred_element_type=jnp.float32)
            * inv_root
        )
        key_pos = offset + jnp.arange(block_size, dtype=jnp.int32)
        if causal:
            allowed = key_pos[None, :] <= query_pos[:, None]
        else:
            allowed = (key_pos < limit)[None, :]
        maxima, totals, weights, factor = refresh(maxima, totals, scores, allowed)
        summed = summed * factor[..., None] + jnp.einsum(
            "kgts,skd->kgtd", weights, value_block, preferred_element_type=jnp.float32
        )
        return (maxima, totals, summed)

    return lax.fori_loop(0, piece_rows // block_size, absorb_step, running)


def on_device(
    stretch_query,
    prefix_keyvals,
    stretch_key_values,
    stretch_start,
    decode_query,
    draft_key_values,
    decode_cache,
    cache_lengths,
    page_rows,
):
    grouped_query = QUERY_HEADS // KEY_VALUE_HEADS
    inv_root = 1.0 / math.sqrt(HEAD_SIZE)
    stretch_rows = stretch_query.shape[1]
    heads_local = stretch_key_values.shape[3] // HEAD_SIZE
    queries = stretch_query[0].reshape(stretch_rows, heads_local, grouped_query, HEAD_SIZE)
    ctx_index = lax.axis_index("ctx")
    query_pos = ctx_index * stretch_rows + jnp.arange(stretch_rows, dtype=jnp.int32)
    limit = stretch_start[0]
    state_shape = (heads_local, grouped_query, stretch_rows)
    running = (
        jnp.full(state_shape, -jnp.inf, jnp.float32),
        jnp.zeros(state_shape, jnp.float32),
        jnp.zeros(state_shape + (HEAD_SIZE,), jnp.float32),
    )
    running = prefill_folder(
        queries,
        query_pos,
        limit,
        False,
        inv_root,
        running,
        lax.all_gather(prefix_keyvals, "ctx", axis=2, tiled=True),
    )
    maxima, totals, summed = prefill_folder(
        queries,
        query_pos,
        limit,
        True,
        inv_root,
        running,
        gather_directly(stretch_key_values, "ctx", 2),
    )
    attended = summed / totals[..., None]
    prefill_out = (
        attended.transpose(2, 0, 1, 3)
        .reshape(1, stretch_rows, heads_local * grouped_query * HEAD_SIZE)
        .astype(jnp.bfloat16)
    )
    within = gather_directly(stretch_key_values, "ctx", 0)
    pages = gather_directly(within, "group", 0)
    row_count = decode_query.shape[0]
    steps = decode_query.shape[1]
    page_size = stretch_key_values.shape[2]
    decode_heads = decode_query.reshape(row_count, steps, heads_local, grouped_query, HEAD_SIZE)
    row_ids = lax.axis_index(("group", "ctx")) * row_count + jnp.arange(row_count, dtype=jnp.int32)
    matches = row_ids[:, None] == page_rows[None, :]
    has_page = jnp.any(matches, axis=1)
    page_block = jnp.einsum(
        "rp,pcsd->crsd", matches.astype(jnp.bfloat16), pages, preferred_element_type=jnp.float32
    ).astype(jnp.bfloat16)
    first_block = jnp.where(
        has_page[None, :, None, None], page_block, decode_cache[:, :, :page_size]
    )

    def absorb(carry, block, allowed):
        maxima, totals, summed = carry
        block_rows = block.shape[2]
        key_block = block[0].reshape(row_count, block_rows, heads_local, HEAD_SIZE)
        value_block = block[1].reshape(row_count, block_rows, heads_local, HEAD_SIZE)
        scores = (
            jnp.einsum(
                "rtkgd,rskd->rkgts", decode_heads, key_block, preferred_element_type=jnp.float32
            )
            * inv_root
        )
        maxima, totals, weights, factor = refresh(maxima, totals, scores, allowed)
        summed = summed * factor[..., None] + jnp.einsum(
            "rkgts,rskd->rkgtd", weights, value_block, preferred_element_type=jnp.float32
        )
        return (maxima, totals, summed)

    def cache_allowed(offset):
        positions = offset + jnp.arange(page_size, dtype=jnp.int32)
        return (positions[None, :] < cache_lengths[:, None])[:, None, None, None, :]

    decode_shape = (row_count, heads_local, grouped_query, steps)
    running = (
        jnp.full(decode_shape, -jnp.inf, jnp.float32),
        jnp.zeros(decode_shape, jnp.float32),
        jnp.zeros(decode_shape + (HEAD_SIZE,), jnp.float32),
    )
    running = absorb(running, first_block, cache_allowed(0))

    def cache_step(block_index, carry):
        offset = block_index * page_size
        block = lax.dynamic_slice_in_dim(decode_cache, offset, page_size, 2)
        return absorb(carry, block, cache_allowed(offset))

    upper = decode_cache.shape[2] // page_size
    running = lax.fori_loop(1, upper, cache_step, running)
    step_pos = jnp.arange(steps, dtype=jnp.int32)
    draft_allowed = (step_pos[None, :] <= step_pos[:, None])[None, None, None, :, :]
    maxima, totals, summed = absorb(running, draft_key_values, draft_allowed)
    decoded = summed / totals[..., None]
    decode_out = (
        decoded.transpose(0, 3, 1, 2, 4)
        .reshape(row_count, steps, heads_local * grouped_query * HEAD_SIZE)
        .astype(jnp.bfloat16)
    )
    return (prefill_out, decode_out)


def solution(mesh):
    return jax.shard_map(
        on_device,
        mesh=mesh,
        in_specs=(
            P("group", "ctx", "tp"),
            P("group", None, "ctx", "tp"),
            P("group", None, "ctx", "tp"),
            P("group"),
            P(("group", "ctx"), None, "tp"),
            P(None, ("group", "ctx"), None, "tp"),
            P(None, ("group", "ctx"), None, "tp"),
            P(("group", "ctx")),
            P(),
        ),
        out_specs=(P("group", "ctx", "tp"), P(("group", "ctx"), None, "tp")),
        check_vma=False,
    )
```

profile of v0, /device:TPU:1, one launch (start us, length us, event | category | flops | bytes accessed | tf_op | source)
XLA Modules:
  0.0 353.9 jit_solution(2781687481947533330)
XLA Ops:
  8.2 33.8 %all_to_all.11 = bf16[16,1,2,128,128]{4,3,2,1,0:T(8,128)(2,1)S(1)} all-to-all(bf16[16,1,2,128,128]{4,3,2,1,0:T(8,128)(2,1)S(1)} %broadcast_in_dim.189), channel_id=1, replica_groups=mesh['group'=2,'ctx'=16,'tp'=8] {'ctx'}, dimensions={0} | all-to-all | bytes 2097152 | tf_op jit(solution)/shard_map/all_to_all | solution.py:20
  44.3 5.6 %all-to-all-start.1 = ((bf16[2,16,2,128,128]{4,1,3,2,0:T(8,128)(2,1)}), bf16[2,16,2,128,128]{4,1,3,2,0:T(8,128)(2,1)}, u32[]{:S(2)}, u32[]{:S(2)}) async-start(bf16[2,16,2,128,128]{4,1,3,2,0:T(8,128)(2,1)} %broadcast_in_dim.192), calls=%async_computation.1 | async-start | bytes 4194304 | tf_op jit(solution)/shard_map/all_to_all | solution.py:20
  53.3 25.6 %all-to-all-done.1 = bf16[2,16,2,128,128]{4,1,3,2,0:T(8,128)(2,1)} async-done(((bf16[2,16,2,128,128]{4,1,3,2,0:T(8,128)(2,1)}), bf16[2,16,2,128,128]{4,1,3,2,0:T(8,128)(2,1)}, u32[]{:S(2)}, u32[]{:S(2)}) %all-to-all-start.1) | async-done | bytes 2097184 | tf_op jit(solution)/shard_map/all_to_all | solution.py:20
  78.9 2.0 copy.47
  83.1 23.9 %while.53 = (s32[]{:T(128)}, f32[16,1,8,4]{2,3,0,1:T(4,128)S(1)}, f32[16,1,8,4]{2,3,0,1:T(4,128)S(1)}, f32[16,1,8,4,128]{4,2,3,0,1:T(8,128)S(1)}, s32[16]{0:T(12...) while((s32[]{:T(128)}, f32[16,1,8,4]{2,3,0,1:T(4,128)S(1)}, ...), condition=%wide.region_14.15_spmd, body=%wide.region_11.14_spmd.sunk | while | flops 34151044 | bytes 2532607 | solution.py:166
  108.2 79.4 %all-gather.2.cloned.1.call-done = bf16[1,2,16384,128]{3,2,1,0:T(8,128)(2,1)} async-done(((bf16[1,2,1024,128]{3,2,1,0:T(8,128)(2,1)}), bf16[1,2,16384,128]{3,2,1,0:T(8,128)(2,1)}) %all-gather.2.cloned.1.call-update) | async-done | bytes 8388624 | tf_op jit(solution)/shard_map/all_gather | solution.py:98
  187.6 144.1 %while.55 = (s32[]{:T(128)}, f32[1,8,128]{2,1,0:T(8,128)S(1)}, f32[1,8,128]{2,1,0:T(8,128)S(1)}, f32[1,8,128,128]{3,2,1,0:T(8,128)S(1)}, s32[]{:T(128)}, /*index...) while((s32[]{:T(128)}, f32[1,8,128]{2,1,0:T(8,128)S(1)}, ...), condition=%wide.region_3.4_spmd.clone, body=%wide.region_0.3_spmd.clone.sunk | while | flops 274609152 | bytes 7940311 | solution.py:63
  194.7 1.9 fusion.123
  203.7 1.9 fusion.123
  212.7 1.9 fusion.123
  217.2 1.9 fusion.123
  226.2 1.9 fusion.123
  230.7 1.9 fusion.123
  244.3 1.9 fusion.123
  253.3 1.9 fusion.123
  257.8 1.9 fusion.123
  271.3 1.9 fusion.123
  280.3 1.9 fusion.123
  284.8 1.9 fusion.123
  298.3 1.9 fusion.123
  307.3 1.9 fusion.123
  311.8 1.9 fusion.123
  325.3 1.9 fusion.123
  331.8 14.1 %while.54 = (s32[]{:T(128)}, f32[1,8,128]{2,1,0:T(8,128)S(1)}, f32[1,8,128]{2,1,0:T(8,128)S(1)}, f32[1,8,128,128]{3,2,1,0:T(8,128)S(1)}, bf16[1,2,2048,128]{3,2,...) while((s32[]{:T(128)}, f32[1,8,128]{2,1,0:T(8,128)S(1)}, ...), condition=%wide.region_7.8_spmd.clone, body=%wide.region_4.7_spmd.clone.sunk | while | flops 272443008 | bytes 8074443 | solution.py:63
  (388 shorter events, 159.7 us)
Async XLA Ops:
  44.3 6.4 %copy-start = (bf16[16,4,1024]{2,1,0:T(4,128)(2,1)S(1)}, bf16[16,4,1024]{2,1,0:T(4,128)(2,1)}, u32[]{:S(2)}) copy-start(bf16[16,4,1024]{2,1,0:T(4,128)(2,1)} %param.19) | copy-start | bytes 393220
  44.3 6.5 %copy-start.1 = (bf16[1,128,1024]{2,1,0:T(8,128)(2,1)S(1)}, bf16[1,128,1024]{2,1,0:T(8,128)(2,1)}, u32[]{:S(2)}) copy-start(bf16[1,128,1024]{2,1,0:T(8,128)(2,1)} %param.15) | copy-start | bytes 786436
  44.3 34.6 %all-to-all-start.1 = ((bf16[2,16,2,128,128]{4,1,3,2,0:T(8,128)(2,1)}), bf16[2,16,2,128,128]{4,1,3,2,0:T(8,128)(2,1)}, u32[]{:S(2)}, u32[]{:S(2)}) async-start(bf16[2,16,2,128,128]{4,1,3,2,0:T(8,128)(2,1)} %broadcast_in_dim.192), calls=%async_computation.1 | async-start | bytes 4194304 | tf_op jit(solution)/shard_map/all_to_all | solution.py:20
  49.9 1.3 copy-start.3
  49.9 1.5 copy-start.2
  49.9 1.6 copy-start.4
  49.9 137.7 %all-gather.2.cloned.1.call-start = ((), (), s32[]{:S(2)}) async-start(), calls=%async_computation.2 | async-start | bytes 8912896 | tf_op jit(solution)/shard_map/all_gather | solution.py:98
  53.3 27.5 %slice-start = ((bf16[2,16,1024,128]{3,2,1,0:T(8,128)(2,1)}), bf16[2,16,128,128]{3,2,1,0:T(8,128)(2,1)S(1)}, s32[]{:S(2)}) async-start(bf16[2,16,1024,128]{3,2,1,0:T(8,128)(2,1)} %param.21), calls=%async_computation.3 | async-start | bytes 2097152 | tf_op jit(solution)/shard_map/slice | solution.py:128
Sparse Core Ops, SparseCore 0:
  52.6 135.0 all-gather.1
where the time goes:
time: 356 us; the launch traced here: 354 us
  matrix products  139 us (39%)
  waiting for transfers between devices  106 us (30%)
  other arithmetic  43.6 us (12%)
  blocking collectives  33.8 us (9%)
  between operations  14.2 us (4%)
  local copies, waits for them, and re-layouts  8.86 us (2%)
  starting transfers between devices  5.65 us (2%)
    all_gather x1, waiting for transfers between devices, on_device(): lax.all_gather(prefix_keyvals, 'ctx', axis=2, tiled=True)  79.4 us
    dot_general x36, matrix products, absorb_step(): jnp.einsum('kgts,skd->kgtd', weights, value_block, preferred_element_type...  66.9 us
    dot_general x36, matrix products, absorb_step(): jnp.einsum('tkgd,skd->kgts', queries, key_block, preferred_element_type=j...  48.8 us
    all_to_all x1, blocking collectives, copy_for_each(): return lax.all_to_all(copies, axis, split_axis=0, concat_axis=0, tiled=True)  33.8 us
    all_to_all x1, waiting for transfers between devices, copy_for_each(): return lax.all_to_all(copies, axis, split_axis=0, concat_axis=0, tiled=True)  25.6 us
    lt x32, other arithmetic, absorb_step(): allowed = (key_pos < limit)[None, :]  20.9 us
    reduce_sum x45, other arithmetic, refresh(): totals = totals * factor + jnp.sum(weights, axis=-1)  19.4 us
    dot_general x9, matrix products, absorb(): jnp.einsum('rtkgd,rskd->rkgts', decode_heads, key_block, preferred_elemen...  11.8 us
  transfers between devices with their start and end apart: 2, of which 2 were waited for; matrix products, arithmetic and copies ran while one was open for 9% of the time, Pallas kernels for 0%

commit v1 on v0

--- a/solution.py
+++ b/solution.py
@@ -95,7 +95,9 @@
         False,
         inv_root,
         running,
-        lax.all_gather(prefix_keyvals, "ctx", axis=2, tiled=True),
+        jnp.concatenate(
+            lax.all_to_all(jnp.stack([prefix_keyvals] * lax.axis_size("ctx")), "ctx", 0, 0), axis=2
+        ),
     )
     maxima, totals, summed = prefill_folder(
         queries,

time: 356 us -> 455 us (1.28)
  the two profiles are of different devices: /device:TPU:1 before, /device:TPU:70 now
where the time goes in v1:
time: 455 us; the launch traced here: 452 us
  waiting for transfers between devices  151 us (33%)
  matrix products  139 us (31%)
  blocking collectives  88.9 us (20%)
  other arithmetic  43.6 us (10%)
  local copies, waits for them, and re-layouts  19.5 us (4%)
  starting transfers between devices  5.87 us (1%)
    all_to_all x1, waiting for transfers between devices, on_device(): lax.all_to_all(jnp.stack([prefix_keyvals] * lax.axis_size('ctx')), 'ctx',...  151 us
    all_to_all x2, blocking collectives, copy_for_each(): return lax.all_to_all(copies, axis, split_axis=0, concat_axis=0, tiled=True)  88.9 us
    dot_general x36, matrix products, absorb_step(): jnp.einsum('kgts,skd->kgtd', weights, value_block, preferred_element_type...  67 us
    dot_general x36, matrix products, absorb_step(): jnp.einsum('tkgd,skd->kgts', queries, key_block, preferred_element_type=j...  48.8 us
    lt x32, other arithmetic, absorb_step(): allowed = (key_pos < limit)[None, :]  20.9 us
    reduce_sum x45, other arithmetic, refresh(): totals = totals * factor + jnp.sum(weights, axis=-1)  19.4 us
    dot_general x9, matrix products, absorb(): jnp.einsum('rtkgd,rskd->rkgts', decode_heads, key_block, preferred_elemen...  11.8 us
    dot_general x9, matrix products, absorb(): jnp.einsum('rkgts,rskd->rkgtd', weights, value_block, preferred_element_t...  10.2 us
  transfers between devices with their start and end apart: 1, of which 1 were waited for; matrix products, arithmetic and copies ran while one was open for 7% of the time, Pallas kernels for 0%

profile of v1, /device:TPU:70, one launch (start us, length us, event | category | flops | bytes accessed | tf_op | source)
XLA Modules:
  0.0 451.8 jit_solution(13590647110242161330)
XLA Ops:
  1.7 33.8 %all_to_all.16 = bf16[16,1,2,128,128]{4,3,2,1,0:T(8,128)(2,1)S(1)} all-to-all(bf16[16,1,2,128,128]{4,3,2,1,0:T(8,128)(2,1)S(1)} %broadcast_in_dim.189), channel_id=1, replica_groups=mesh['group'=2,'ctx'=16,'tp'=8] {'ctx'}, dimensions={0} | all-to-all | bytes 2097152 | tf_op jit(solution)/shard_map/all_to_all | solution.py:20
  36.4 55.2 %all_to_all.17 = bf16[2,16,2,128,128]{4,1,3,2,0:T(8,128)(2,1)} all-to-all(bf16[2,16,2,128,128]{4,1,3,2,0:T(8,128)(2,1)S(1)} %broadcast_in_dim.192), channel_id=1, replica_groups=mesh['group'=2,'ctx'=16,'tp'=8] {'group'}, dimensions={0} | all-to-all | bytes 4194304 | tf_op jit(solution)/shard_map/all_to_all | solution.py:20
  91.6 5.2 %stack.2 = bf16[16,1,2,1024,128]{4,3,2,1,0:T(8,128)(2,1)} broadcast(bf16[2,1024,128]{2,1,0:T(8,128)(2,1)S(1)} %bitcast.321), dimensions={2,3,4} | broadcast | bytes 8912896 | tf_op jit(solution)/shard_map/stack | solution.py:99
  96.8 5.9 %all-to-all-start = ((bf16[16,1,2,1024,128]{4,3,2,1,0:T(8,128)(2,1)}), bf16[16,1,2,1024,128]{4,3,2,1,0:T(8,128)(2,1)}, u32[]{:S(2)}, u32[]{:S(2)}) async-start(bf16[16,1,2,1024,128]{4,3,2,1,0:T(8,128)(2,1)} %stack.2), calls=%async_computation | async-start | bytes 16777216 | tf_op jit(solution)/shard_map/all_to_all | solution.py:99
  108.8 23.8 %while.53 = (s32[]{:T(128)}, f32[16,1,8,4]{2,3,0,1:T(4,128)S(1)}, f32[16,1,8,4]{2,3,0,1:T(4,128)S(1)}, f32[16,1,8,4,128]{4,2,3,0,1:T(8,128)S(1)}, s32[16]{0:T(12...) while((s32[]{:T(128)}, f32[16,1,8,4]{2,3,0,1:T(4,128)S(1)}, ...), condition=%wide.region_14.15_spmd, body=%wide.region_11.14_spmd.sunk | while | flops 34151044 | bytes 2532607 | solution.py:168
  133.9 150.9 %all-to-all-done = bf16[16,1,2,1024,128]{4,3,2,1,0:T(8,128)(2,1)} async-done(((bf16[16,1,2,1024,128]{4,3,2,1,0:T(8,128)(2,1)}), bf16[16,1,2,1024,128]{4,3,2,1,0:T(8,128)(2,1)}, u32[]{:S(2)}, u32[]{:S(2)}) %all-to-all-start) | async-done | bytes 8388640 | tf_op jit(solution)/shard_map/all_to_all | solution.py:99
  284.8 7.5 %copy.41 = bf16[16,1,2,1024,128]{4,3,0,2,1:T(8,128)(2,1)} copy(bf16[16,1,2,1024,128]{4,3,2,1,0:T(8,128)(2,1)} %all-to-all-done) | data formatting | bytes 16777216 | tf_op jit(solution)/shard_map/all_to_all | solution.py:99
  292.3 144.1 %while.55 = (s32[]{:T(128)}, f32[1,8,128]{2,1,0:T(8,128)S(1)}, f32[1,8,128]{2,1,0:T(8,128)S(1)}, f32[1,8,128,128]{3,2,1,0:T(8,128)S(1)}, s32[]{:T(128)}, /*index...) while((s32[]{:T(128)}, f32[1,8,128]{2,1,0:T(8,128)S(1)}, ...), condition=%wide.region_3.4_spmd.clone, body=%wide.region_0.3_spmd.clone.sunk | while | flops 274609152 | bytes 7940311 | solution.py:63
  294.9 1.9 fusion.123
  299.4 1.9 fusion.123
  308.4 1.9 fusion.123
  312.9 1.9 fusion.123
  321.9 1.9 fusion.123
  326.4 1.9 fusion.123
  340.0 1.9 fusion.123
  349.0 1.9 fusion.123
  353.5 1.9 fusion.123
  367.0 1.9 fusion.123
  380.5 1.9 fusion.123
  394.0 1.9 fusion.123
  407.5 1.9 fusion.123
  421.1 1.9 fusion.123
  434.6 1.9 fusion.123
  436.5 14.1 %while.54 = (s32[]{:T(128)}, f32[1,8,128]{2,1,0:T(8,128)S(1)}, f32[1,8,128]{2,1,0:T(8,128)S(1)}, f32[1,8,128,128]{3,2,1,0:T(8,128)S(1)}, bf16[1,2,2048,128]{3,2,...) while((s32[]{:T(128)}, f32[1,8,128]{2,1,0:T(8,128)S(1)}, ...), condition=%wide.region_7.8_spmd.clone, body=%wide.region_4.7_spmd.clone.sunk | while | flops 272443008 | bytes 8074443 | solution.py:63
  (392 shorter events, 160.8 us)
Async XLA Ops:
  36.4 55.2 %copy-start.1 = (bf16[1,2,1024,128]{3,2,1,0:T(8,128)(2,1)S(1)}, bf16[1,2,1024,128]{3,2,1,0:T(8,128)(2,1)}, u32[]{:S(2)}) copy-start(bf16[1,2,1024,128]{3,2,1,0:T(8,128)(2,1)} %param.16) | copy-start | bytes 1572868
  96.8 5.9 %copy-start.2 = (bf16[16,4,1024]{2,1,0:T(4,128)(2,1)S(1)}, bf16[16,4,1024]{2,1,0:T(4,128)(2,1)}, u32[]{:S(2)}) copy-start(bf16[16,4,1024]{2,1,0:T(4,128)(2,1)} %param.19) | copy-start | bytes 393220
  96.8 6.1 %copy-start.3 = (bf16[1,128,1024]{2,1,0:T(8,128)(2,1)S(1)}, bf16[1,128,1024]{2,1,0:T(8,128)(2,1)}, u32[]{:S(2)}) copy-start(bf16[1,128,1024]{2,1,0:T(8,128)(2,1)} %param.15) | copy-start | bytes 786436
  96.8 188.0 %all-to-all-start = ((bf16[16,1,2,1024,128]{4,3,2,1,0:T(8,128)(2,1)}), bf16[16,1,2,1024,128]{4,3,2,1,0:T(8,128)(2,1)}, u32[]{:S(2)}, u32[]{:S(2)}) async-start(bf16[16,1,2,1024,128]{4,3,2,1,0:T(8,128)(2,1)} %stack.2), calls=%async_computation | async-start | bytes 16777216 | tf_op jit(solution)/shard_map/all_to_all | solution.py:99
  102.6 0.7 copy-start.5
  102.7 0.8 copy-start.4
  102.7 0.9 copy-start.6
  103.2 2.1 copy-start
  105.3 1.2 slice-start
